TPU v7x, 32 devices: a whole 2x2x4 slice. The times are simulated.
32 devices in a mesh: groups: 2 (over x), ctx: 16 (over z, y, core).
Axes of the slice: x: 2, y: 2, z: 4, core: 2. Of those that a mesh axis runs over, the one named last changes fastest.
Arguments:
- query_video: bfloat16 [12288, 1536], P(('groups', 'ctx')), parts along dimension 0, may hold values from -10 to 10
- key_video: bfloat16 [12288, 1536], P(('groups', 'ctx')), parts along dimension 0, may hold values from -5 to 5
- value_video: bfloat16 [12288, 1536], P(('groups', 'ctx')), parts along dimension 0, may hold values from -6 to 6
- query_text: bfloat16 [512, 1536], P(('groups', 'ctx')), parts along dimension 0, may hold values from -10 to 10
- key_text: bfloat16 [512, 1536], P(('groups', 'ctx')), parts along dimension 0, may hold values from -5 to 5
- value_text: bfloat16 [512, 1536], P(('groups', 'ctx')), parts along dimension 0, may hold values from -6 to 6
- key_tiles: int32 [32, 3], P(('groups', 'ctx')), parts along dimension 0, may hold values from 0 to 15, as said below
- tile_owner: int32 [32], P('groups'), parts along dimension 0, may hold values from 0 to 15, as said below
- text_count: int32 [2], P('groups'), parts along dimension 0, may hold values from 64 to 256
Outputs:
- video_out: bfloat16 [12288, 1536], P(('groups', 'ctx')), parts along dimension 0
- text_out: bfloat16 [512, 1536], P(('groups', 'ctx')), parts along dimension 0
There are 2 independent parts, one for each index of `groups`. A program takes and returns all parts, laid end to end along the dimension named above; each array names one. Nothing has to cross between parts.
Inputs may be any that keep to these rules, and one draw needn't show every extreme that they name: `key_tiles`: each list names 3 different tiles, the query tile itself among them; every listed tile has a stored position whose device (position) is at most 2 away from the query tile's device, and every list names one exactly 2 away. `tile_owner`: A permutation of the tile numbers.
All inputs are finite; a program needn't handle non-finite values.
Results may differ from a plain program's by a relative error of at most 0.0032.
Values may be sent and summed in bfloat16 or wider, within the bound.
A program may use at most 384 MiB of HBM per device.

v0:
```python
import math
import jax
import jax.numpy as jnp
from jax import lax
from jax.sharding import PartitionSpec as P

TILE = 384
HD = 128
NB = 3
REACH = 2


def shifted(shard, axis, by):
    count = lax.axis_size(axis)
    pairs = [(i, i + by) for i in range(count) if 0 <= i + by < count]
    return lax.ppermute(shard, axis, pairs)


def combined_all(value, axis, join):
    pieces = jax.tree.map(lambda part: lax.all_gather(part, axis), value)
    head = jax.tree.map(lambda part: part[0], pieces)
    tail = jax.tree.map(lambda part: part[1:], pieces)
    total, _ = lax.scan(lambda total, share: (join(total, share), None), head, tail)
    return total


def spread_heads(values):
    return jnp.repeat(values, HD, axis=1)


def combine_parts(earlier_part, later_part):
    max_early, total_early, acc_early = earlier_part
    max_late, total_late, acc_late = later_part
    joint_max = jnp.maximum(max_early, max_late)
    factor_early = jnp.exp(max_early - joint_max)
    factor_late = jnp.exp(max_late - joint_max)
    joint_total = total_early * factor_early + total_late * factor_late
    joint_acc = acc_early * spread_heads(factor_early) + acc_late * spread_heads(factor_late)
    return (joint_max, joint_total, joint_acc)


def on_device(
    query_video,
    key_video,
    value_video,
    query_text,
    key_text,
    value_text,
    key_tiles,
    tile_owner,
    text_count,
):
    ctx_rank = lax.axis_index("ctx")
    row_count, feature_width = query_video.shape
    head_count = feature_width // HD
    tiles_here = row_count // TILE
    text_here = query_text.shape[0]
    inverse_root_dimension = 1.0 / math.sqrt(HD)
    text_query, text_keys, text_values = (
        lax.all_gather(query_text, "ctx", axis=0, tiled=True),
        lax.all_gather(key_text, "ctx", axis=0, tiled=True),
        lax.all_gather(value_text, "ctx", axis=0, tiled=True),
    )
    text_rows = text_keys.shape[0]
    text_limit = text_count[0]
    text_ok = jnp.arange(text_rows) < text_limit
    local_ok = ctx_rank * text_here + jnp.arange(text_here) < text_limit
    own_pair = (key_video, value_video)
    fetched = {}
    for offset in [value for value in range(-REACH, REACH + 1) if value != 0]:
        fetched[offset] = shifted((own_pair[0], own_pair[1]), "ctx", -offset)
    fetched[0] = own_pair
    window_keys = jnp.concatenate(
        [fetched[offset][0] for offset in range(-REACH, REACH + 1)], axis=0
    )
    window_values = jnp.concatenate(
        [fetched[offset][1] for offset in range(-REACH, REACH + 1)], axis=0
    )
    window_tiles = (2 * REACH + 1) * tiles_here
    tile_count = tile_owner.shape[0]
    matches = key_tiles[:, :, None] == jnp.arange(tile_count, dtype=jnp.int32)[None, None, :]
    key_slots = jnp.sum(jnp.where(matches, tile_owner[None, None, :], 0), axis=-1)
    window_index = key_slots - (ctx_rank - REACH) * tiles_here

    def head_step(head_index, carry_state):
        video_buffer, text_max, text_sum, text_acc = carry_state
        column_start = head_index * HD
        query_head = lax.dynamic_slice_in_dim(query_video, column_start, HD, 1).reshape(
            tiles_here, TILE, HD
        )
        key_window = lax.dynamic_slice_in_dim(window_keys, column_start, HD, 1).reshape(
            window_tiles, TILE, HD
        )
        value_window = lax.dynamic_slice_in_dim(window_values, column_start, HD, 1).reshape(
            window_tiles, TILE, HD
        )
        key_near = key_window[window_index].reshape(tiles_here, NB * TILE, HD)
        value_near = value_window[window_index].reshape(tiles_here, NB * TILE, HD)
        key_words = lax.dynamic_slice_in_dim(text_keys, column_start, HD, 1)
        value_words = lax.dynamic_slice_in_dim(text_values, column_start, HD, 1)
        frame_affinity_array = (
            jnp.einsum("tqd,tkd->tqk", query_head, key_near, preferred_element_type=jnp.float32)
            * inverse_root_dimension
        )
        wording_affinity_array = (
            jnp.einsum("tqd,kd->tqk", query_head, key_words, preferred_element_type=jnp.float32)
            * inverse_root_dimension
        )
        wording_affinity_array = jnp.where(text_ok[None, None, :], wording_affinity_array, -jnp.inf)
        row_max = jnp.maximum(
            jnp.max(frame_affinity_array, axis=-1, keepdims=True),
            jnp.max(wording_affinity_array, axis=-1, keepdims=True),
        )
        weight_video = jnp.exp(frame_affinity_array - row_max)
        weight_text = jnp.exp(wording_affinity_array - row_max)
        row_total = jnp.sum(weight_video, axis=-1) + jnp.sum(weight_text, axis=-1)
        mixed_values = jnp.einsum(
            "tqk,tkd->tqd",
            weight_video.astype(jnp.bfloat16),
            value_near,
            preferred_element_type=jnp.float32,
        )
        mixed_values = mixed_values + jnp.einsum(
            "tqk,kd->tqd",
            weight_text.astype(jnp.bfloat16),
            value_words,
            preferred_element_type=jnp.float32,
        )
        head_output = (
            (mixed_values / row_total[:, :, None]).astype(jnp.bfloat16).reshape(row_count, HD)
        )
        video_buffer = lax.dynamic_update_slice_in_dim(video_buffer, head_output, column_start, 1)
        text_head = lax.dynamic_slice_in_dim(text_query, column_start, HD, 1)
        key_local = lax.dynamic_slice_in_dim(key_video, column_start, HD, 1)
        value_local = lax.dynamic_slice_in_dim(value_video, column_start, HD, 1)
        key_own_text = lax.dynamic_slice_in_dim(key_text, column_start, HD, 1)
        value_own_text = lax.dynamic_slice_in_dim(value_text, column_start, HD, 1)
        score_local = (
            jnp.einsum("td,kd->tk", text_head, key_local, preferred_element_type=jnp.float32)
            * inverse_root_dimension
        )
        score_own = (
            jnp.einsum("td,kd->tk", text_head, key_own_text, preferred_element_type=jnp.float32)
            * inverse_root_dimension
        )
        score_own = jnp.where(local_ok[None, :], score_own, -jnp.inf)
        block_max = jnp.maximum(jnp.max(score_local, axis=-1), jnp.max(score_own, axis=-1))
        weight_local = jnp.exp(score_local - block_max[:, None])
        weight_own = jnp.exp(score_own - block_max[:, None])
        block_total = jnp.sum(weight_local, axis=-1) + jnp.sum(weight_own, axis=-1)
        block_acc = jnp.einsum(
            "tk,kd->td",
            weight_local.astype(jnp.bfloat16),
            value_local,
            preferred_element_type=jnp.float32,
        )
        block_acc = block_acc + jnp.einsum(
            "tk,kd->td",
            weight_own.astype(jnp.bfloat16),
            value_own_text,
            preferred_element_type=jnp.float32,
        )
        text_max = lax.dynamic_update_slice(text_max, block_max[:, None], (0, head_index))
        text_sum = lax.dynamic_update_slice(text_sum, block_total[:, None], (0, head_index))
        text_acc = lax.dynamic_update_slice_in_dim(text_acc, block_acc, column_start, 1)
        return (video_buffer, text_max, text_sum, text_acc)

    initial_state = (
        jnp.zeros((row_count, feature_width), jnp.bfloat16),
        jnp.zeros((text_rows, head_count), jnp.float32),
        jnp.zeros((text_rows, head_count), jnp.float32),
        jnp.zeros((text_rows, feature_width), jnp.float32),
    )
    video_out, text_max, text_sum, text_acc = lax.fori_loop(0, head_count, head_step, initial_state)
    joint_max, joint_total, joint_acc = combined_all(
        (text_max, text_sum, text_acc), "ctx", combine_parts
    )
    own_total = lax.dynamic_slice_in_dim(joint_total, ctx_rank * text_here, text_here, 0)
    own_acc = lax.dynamic_slice_in_dim(joint_acc, ctx_rank * text_here, text_here, 0)
    text_out = (own_acc / spread_heads(own_total)).astype(jnp.bfloat16)
    return (video_out, text_out)


def solution(mesh):
    return jax.shard_map(
        on_device,
        mesh=mesh,
        in_specs=(
            P(("groups", "ctx"), None),
            P(("groups", "ctx"), None),
            P(("groups", "ctx"), None),
            P(("groups", "ctx"), None),
            P(("groups", "ctx"), None),
            P(("groups", "ctx"), None),
            P(("groups", "ctx"), None),
            P("groups"),
            P("groups"),
        ),
        out_specs=(P(("groups", "ctx"), None), P(("groups", "ctx"), None)),
        check_vma=False,
    )
```

profile of v0, /device:TPU:0, one launch (start us, length us, event | category | flops | bytes accessed | tf_op | source)
XLA Modules:
  0.0 659.5 jit_solution(15291442228963987204)
XLA Ops:
  7.3 6.1 collective-permute-start
  13.3 2.5 collective-permute-start.1
  17.1 5.3 collective-permute-start.4
  22.3 2.6 collective-permute-start.5
  24.9 93.3 %all_gather.27 = bf16[256,1536]{1,0:T(8,128)(2,1)S(1)} all-gather(bf16[16,1536]{1,0:T(8,128)(2,1)} %param.17), channel_id=1, replica_groups=mesh['groups'=2,'ctx'=16] {'ctx'}, dimensions={0}, use_global_device_ids=true | all-gather | bytes 835584 | tf_op jit(solution)/shard_map/all_gather | solution.py:61
  118.2 24.4 %all_gather.28 = bf16[256,1536]{1,0:T(8,128)(2,1)} all-gather(bf16[16,1536]{1,0:T(8,128)(2,1)} %param.18), channel_id=1, replica_groups=mesh['groups'=2,'ctx'=16] {'ctx'}, dimensions={0}, use_global_device_ids=true | all-gather | bytes 835584 | tf_op jit(solution)/shard_map/all_gather | solution.py:62
  142.6 21.0 %all_gather.29 = bf16[256,1536]{1,0:T(8,128)(2,1)} all-gather(bf16[16,1536]{1,0:T(8,128)(2,1)S(1)} %copy-done.12), channel_id=1, replica_groups=mesh['groups'=2,'ctx'=16] {'ctx'}, dimensions={0}, use_global_device_ids=true | all-gather | bytes 835584 | tf_op jit(solution)/shard_map/all_gather | solution.py:60
  174.7 19.8 %collective-permute-done.3 = bf16[384,1536]{1,0:T(8,128)(2,1)S(1)} collective-permute-done((bf16[384,1536]{1,0:T(8,128)(2,1)S(1)}, bf16[384,1536]{1,0:T(8,128)(2,1)S(1)}, u32[]{:S(2)}, u32[]{:S(2)}) %collective-permute-start.3) | collective-permute-done | bytes 1179680 | tf_op jit(solution)/shard_map/ppermute | solution.py:16
  194.7 37.3 %collective-permute-done.7 = bf16[384,1536]{1,0:T(8,128)(2,1)S(1)} collective-permute-done((bf16[384,1536]{1,0:T(8,128)(2,1)}, bf16[384,1536]{1,0:T(8,128)(2,1)S(1)}, u32[]{:S(2)}, u32[]{:S(2)}) %collective-permute-start.7) | collective-permute-done | bytes 1179680 | tf_op jit(solution)/shard_map/ppermute | solution.py:16
  235.4 179.9 %while.36 = (s32[]{:T(128)}, bf16[384,1536]{1,0:T(8,128)(2,1)}, f32[256,12]{0,1:T(8,128)S(1)}, f32[256,12]{0,1:T(8,128)S(1)}, f32[256,1536]{1,0:T(8,128)}, /*ind...) while((s32[]{:T(128)}, bf16[384,1536]{1,0:T(8,128)(2,1)}, ...), condition=%wide.region_10.11_spmd.clone.clone, body=%wide.region_1.10_spmd.clone.clone.sunk | while | flops 333393952 | bytes 24062668 | solution.py:174
  242.4 1.9 fusion.103
  257.4 1.9 fusion.103
  263.1 1.9 fusion.109
  272.4 1.9 fusion.103
  287.4 1.9 fusion.103
  302.4 1.9 fusion.103
  317.4 1.9 fusion.103
  332.4 1.9 fusion.103
  347.4 1.9 fusion.103
  353.1 1.9 fusion.109
  362.4 1.9 fusion.103
  368.1 1.9 fusion.109
  377.4 1.9 fusion.103
  392.4 1.9 fusion.103
  398.1 1.9 fusion.109
  407.4 1.9 fusion.103
  413.1 1.9 fusion.109
  415.4 21.2 %all-gather = f32[4096,12]{0,1:T(8,128)S(1)} all-gather(f32[256,12]{0,1:T(8,128)S(1)} %get-tuple-element.794), channel_id=2, replica_groups=mesh['groups'=2,'ctx'=16] {'ctx'}, dimensions={0}, use_global_device_ids=true | all-gather | bytes 208896 | tf_op jit(solution)/shard_map/all_gather | solution.py:20
  436.6 19.5 %all-gather.1 = f32[4096,12]{0,1:T(8,128)S(1)} all-gather(f32[256,12]{0,1:T(8,128)S(1)} %get-tuple-element.795), channel_id=3, replica_groups=mesh['groups'=2,'ctx'=16] {'ctx'}, dimensions={0}, use_global_device_ids=true | all-gather | bytes 208896 | tf_op jit(solution)/shard_map/all_gather | solution.py:20
  456.2 90.8 %all-gather.5.cloned.1.call-done = f32[4096,1536]{1,0:T(8,128)} async-done(((f32[256,1536]{1,0:T(8,128)}), f32[4096,1536]{1,0:T(8,128)}) %all-gather.5.cloned.1.call-update) | async-done | bytes 25165840 | tf_op jit(solution)/shard_map/all_gather | solution.py:20
  550.0 16.3 %slice.39 = f32[3840,1536]{1,0:T(8,128)} slice(f32[4096,1536]{1,0:T(8,128)} %all-gather.5.cloned.1.call-done), slice={[256:4096], [0:1536]} | slice | bytes 47185920 | tf_op jit(solution)/shard_map/slice | solution.py:22
  566.3 83.5 %while.35 = (s32[]{:T(128)}, f32[256,12]{0,1:T(8,128)S(1)}, f32[256,12]{0,1:T(8,128)S(1)}, f32[256,1536]{0,1:T(8,128)}, f32[15,256,12]{1,0,2:T(8,128)S(1)}, /*in...) while((s32[]{:T(128)}, f32[256,12]{0,1:T(8,128)S(1)}, f32[256,12]{0,1:T(8,128)S(1)}, ...), condition=%wide.region_12.13_spmd, body=%wide.region_11.12_spmd.sunk | while | flops 1198082 | bytes 14131405 | solution.py:23
  569.1 2.8 fusion.87
  574.6 2.8 fusion.87
  580.2 2.8 fusion.87
  585.8 2.8 fusion.87
  591.4 2.8 fusion.87
  596.9 2.8 fusion.87
  602.5 2.8 fusion.87
  608.1 2.8 fusion.87
  613.6 2.8 fusion.87
  619.2 2.8 fusion.87
  624.8 2.8 fusion.87
  630.3 2.8 fusion.87
  635.9 2.8 fusion.87
  641.5 2.8 fusion.87
  647.0 2.8 fusion.87
  650.0 1.9 copy.26
  (594 shorter events, 206.5 us)
Async XLA Ops:
  7.2 156.7 %copy-start = (bf16[384,1536]{1,0:T(8,128)(2,1)S(1)}, bf16[384,1536]{1,0:T(8,128)(2,1)}, u32[]{:S(2)}) copy-start(bf16[384,1536]{1,0:T(8,128)(2,1)} %param.14) | copy-start | bytes 3538948
  7.2 135.4 %copy-start.12 = (bf16[16,1536]{1,0:T(8,128)(2,1)S(1)}, bf16[16,1536]{1,0:T(8,128)(2,1)}, u32[]{:S(2)}) copy-start(bf16[16,1536]{1,0:T(8,128)(2,1)} %param.16) | copy-start | bytes 147460
  7.2 156.4 %copy-start.13 = (s32[1,3]{1,0:T(1,128)S(1)}, s32[1,3]{1,0:T(1,128)}, u32[]{:S(2)}) copy-start(s32[1,3]{1,0:T(1,128)} %param.19) | copy-start | bytes 40
  7.2 156.4 %copy-start.14 = (s32[16]{0:T(128)S(1)}, s32[16]{0:T(128)}, u32[]{:S(2)}) copy-start(s32[16]{0:T(128)} %param.20) | copy-start | bytes 196
  7.2 539.8 %all-gather.5.cloned.1.call-start = ((), (), s32[]{:S(2)}) async-start(), calls=%async_computation | async-start | bytes 26738688 | tf_op jit(solution)/shard_map/all_gather | solution.py:20
  7.3 156.6 %collective-permute-start = (bf16[384,1536]{1,0:T(8,128)(2,1)}, bf16[384,1536]{1,0:T(8,128)(2,1)}, u32[]{:S(2)}, u32[]{:S(2)}) collective-permute-start(bf16[384,1536]{1,0:T(8,128)(2,1)} %param.14), channel_id=1, source_target_pairs={{0,2},{1,3},{2,4},{3,5},{4,6},{5,7},{6,8},{7,9},{8,10},{9,11},{10,... | collective-permute-start | bytes 3538952 | tf_op jit(solution)/shard_map/ppermute | solution.py:16
  13.3 153.2 %collective-permute-start.1 = (bf16[384,1536]{1,0:T(8,128)(2,1)}, bf16[384,1536]{1,0:T(8,128)(2,1)}, u32[]{:S(2)}, u32[]{:S(2)}) collective-permute-start(bf16[384,1536]{1,0:T(8,128)(2,1)} %param.14), channel_id=1, source_target_pairs={{0,1},{1,2},{2,3},{3,4},{4,5},{5,6},{6,7},{7,8},{8,9},{9,10},{10,1... | collective-permute-start | bytes 3538952 | tf_op jit(solution)/shard_map/ppermute | solution.py:16
  15.8 158.8 %collective-permute-start.2 = (bf16[384,1536]{1,0:T(8,128)(2,1)}, bf16[384,1536]{1,0:T(8,128)(2,1)S(1)}, u32[]{:S(2)}, u32[]{:S(2)}) collective-permute-start(bf16[384,1536]{1,0:T(8,128)(2,1)} %param.14), channel_id=1, source_target_pairs={{1,0},{2,1},{3,2},{4,3},{5,4},{6,5},{7,6},{8,7},{9,8},{10,9},{11,1... | collective-permute-start | bytes 3538952 | tf_op jit(solution)/shard_map/ppermute | solution.py:16
  17.1 152.2 %collective-permute-start.4 = (bf16[384,1536]{1,0:T(8,128)(2,1)}, bf16[384,1536]{1,0:T(8,128)(2,1)}, u32[]{:S(2)}, u32[]{:S(2)}) collective-permute-start(bf16[384,1536]{1,0:T(8,128)(2,1)} %param.15), channel_id=1, source_target_pairs={{0,2},{1,3},{2,4},{3,5},{4,6},{5,7},{6,8},{7,9},{8,10},{9,11},{10,... | collective-permute-start | bytes 3538952 | tf_op jit(solution)/shard_map/ppermute | solution.py:16
  22.3 149.6 %collective-permute-start.5 = (bf16[384,1536]{1,0:T(8,128)(2,1)}, bf16[384,1536]{1,0:T(8,128)(2,1)}, u32[]{:S(2)}, u32[]{:S(2)}) collective-permute-start(bf16[384,1536]{1,0:T(8,128)(2,1)} %param.15), channel_id=1, source_target_pairs={{0,1},{1,2},{2,3},{3,4},{4,5},{5,6},{6,7},{7,8},{8,9},{9,10},{10,1... | collective-permute-start | bytes 3538952 | tf_op jit(solution)/shard_map/ppermute | solution.py:16
  163.8 30.7 %collective-permute-start.3 = (bf16[384,1536]{1,0:T(8,128)(2,1)S(1)}, bf16[384,1536]{1,0:T(8,128)(2,1)S(1)}, u32[]{:S(2)}, u32[]{:S(2)}) collective-permute-start(bf16[384,1536]{1,0:T(8,128)(2,1)S(1)} %copy-done), channel_id=1, source_target_pairs={{2,0},{3,1},{4,2},{5,3},{6,4},{7,5},{8,6},{9,7},{10,8},{11,9},{12,... | collective-permute-start | bytes 3538952 | tf_op jit(solution)/shard_map/ppermute | solution.py:16
  166.5 28.1 %collective-permute-start.6 = (bf16[384,1536]{1,0:T(8,128)(2,1)}, bf16[384,1536]{1,0:T(8,128)(2,1)S(1)}, u32[]{:S(2)}, u32[]{:S(2)}) collective-permute-start(bf16[384,1536]{1,0:T(8,128)(2,1)} %param.15), channel_id=1, source_target_pairs={{1,0},{2,1},{3,2},{4,3},{5,4},{6,5},{7,6},{8,7},{9,8},{10,9},{11,1... | collective-permute-start | bytes 3538952 | tf_op jit(solution)/shard_map/ppermute | solution.py:16
  169.2 62.7 %collective-permute-start.7 = (bf16[384,1536]{1,0:T(8,128)(2,1)}, bf16[384,1536]{1,0:T(8,128)(2,1)S(1)}, u32[]{:S(2)}, u32[]{:S(2)}) collective-permute-start(bf16[384,1536]{1,0:T(8,128)(2,1)} %param.15), channel_id=1, source_target_pairs={{2,0},{3,1},{4,2},{5,3},{6,4},{7,5},{8,6},{9,7},{10,8},{11,9},{12,... | collective-permute-start | bytes 3538952 | tf_op jit(solution)/shard_map/ppermute | solution.py:16
  194.6 40.7 %copy-start.2 = (bf16[1920,1536]{1,0:T(8,128)(2,1)}, bf16[1920,1536]{1,0:T(8,128)(2,1)S(1)}, u32[]{:S(2)}) copy-start(bf16[1920,1536]{1,0:T(8,128)(2,1)S(1)} %constant_dynamic-update-slice_fusion) | copy-start | bytes 17694724
  242.4 7.9 %copy-start.1 = (bf16[384,1536]{1,0:T(8,128)(2,1)S(1)}, bf16[384,1536]{1,0:T(8,128)(2,1)}, u32[]{:S(2)}) copy-start(bf16[384,1536]{1,0:T(8,128)(2,1)} %get-tuple-element.814) | copy-start | bytes 3538948 | tf_op jit(solution)/shard_map/while
  242.4 7.9 %copy-start.5 = (bf16[256,1536]{1,0:T(8,128)(2,1)S(1)}, bf16[256,1536]{1,0:T(8,128)(2,1)}, u32[]{:S(2)}) copy-start(bf16[256,1536]{1,0:T(8,128)(2,1)} %copy-done.4) | copy-start | bytes 2359300 | tf_op jit(solution)/shard_map/while
  257.4 8.0 %copy-start.1 = (bf16[384,1536]{1,0:T(8,128)(2,1)S(1)}, bf16[384,1536]{1,0:T(8,128)(2,1)}, u32[]{:S(2)}) copy-start(bf16[384,1536]{1,0:T(8,128)(2,1)} %get-tuple-element.814) | copy-start | bytes 3538948 | tf_op jit(solution)/shard_map/while
  257.4 8.0 %copy-start.5 = (bf16[256,1536]{1,0:T(8,128)(2,1)S(1)}, bf16[256,1536]{1,0:T(8,128)(2,1)}, u32[]{:S(2)}) copy-start(bf16[256,1536]{1,0:T(8,128)(2,1)} %copy-done.4) | copy-start | bytes 2359300 | tf_op jit(solution)/shard_map/while
  265.4 4.3 copy-start.4
  272.4 8.0 %copy-start.1 = (bf16[384,1536]{1,0:T(8,128)(2,1)S(1)}, bf16[384,1536]{1,0:T(8,128)(2,1)}, u32[]{:S(2)}) copy-start(bf16[384,1536]{1,0:T(8,128)(2,1)} %get-tuple-element.814) | copy-start | bytes 3538948 | tf_op jit(solution)/shard_map/while
  272.4 8.0 %copy-start.5 = (bf16[256,1536]{1,0:T(8,128)(2,1)S(1)}, bf16[256,1536]{1,0:T(8,128)(2,1)}, u32[]{:S(2)}) copy-start(bf16[256,1536]{1,0:T(8,128)(2,1)} %copy-done.4) | copy-start | bytes 2359300 | tf_op jit(solution)/shard_map/while
  280.4 4.3 copy-start.4
  287.4 7.9 %copy-start.1 = (bf16[384,1536]{1,0:T(8,128)(2,1)S(1)}, bf16[384,1536]{1,0:T(8,128)(2,1)}, u32[]{:S(2)}) copy-start(bf16[384,1536]{1,0:T(8,128)(2,1)} %get-tuple-element.814) | copy-start | bytes 3538948 | tf_op jit(solution)/shard_map/while
  287.4 7.9 %copy-start.5 = (bf16[256,1536]{1,0:T(8,128)(2,1)S(1)}, bf16[256,1536]{1,0:T(8,128)(2,1)}, u32[]{:S(2)}) copy-start(bf16[256,1536]{1,0:T(8,128)(2,1)} %copy-done.4) | copy-start | bytes 2359300 | tf_op jit(solution)/shard_map/while
  295.4 4.3 copy-start.4
  302.4 7.9 %copy-start.1 = (bf16[384,1536]{1,0:T(8,128)(2,1)S(1)}, bf16[384,1536]{1,0:T(8,128)(2,1)}, u32[]{:S(2)}) copy-start(bf16[384,1536]{1,0:T(8,128)(2,1)} %get-tuple-element.814) | copy-start | bytes 3538948 | tf_op jit(solution)/shard_map/while
  302.4 7.9 %copy-start.5 = (bf16[256,1536]{1,0:T(8,128)(2,1)S(1)}, bf16[256,1536]{1,0:T(8,128)(2,1)}, u32[]{:S(2)}) copy-start(bf16[256,1536]{1,0:T(8,128)(2,1)} %copy-done.4) | copy-start | bytes 2359300 | tf_op jit(solution)/shard_map/while
  317.4 7.9 %copy-start.1 = (bf16[384,1536]{1,0:T(8,128)(2,1)S(1)}, bf16[384,1536]{1,0:T(8,128)(2,1)}, u32[]{:S(2)}) copy-start(bf16[384,1536]{1,0:T(8,128)(2,1)} %get-tuple-element.814) | copy-start | bytes 3538948 | tf_op jit(solution)/shard_map/while
  317.4 7.9 %copy-start.5 = (bf16[256,1536]{1,0:T(8,128)(2,1)S(1)}, bf16[256,1536]{1,0:T(8,128)(2,1)}, u32[]{:S(2)}) copy-start(bf16[256,1536]{1,0:T(8,128)(2,1)} %copy-done.4) | copy-start | bytes 2359300 | tf_op jit(solution)/shard_map/while
  325.3 4.3 copy-start.4
  332.4 7.9 %copy-start.1 = (bf16[384,1536]{1,0:T(8,128)(2,1)S(1)}, bf16[384,1536]{1,0:T(8,128)(2,1)}, u32[]{:S(2)}) copy-start(bf16[384,1536]{1,0:T(8,128)(2,1)} %get-tuple-element.814) | copy-start | bytes 3538948 | tf_op jit(solution)/shard_map/while
  332.4 7.9 %copy-start.5 = (bf16[256,1536]{1,0:T(8,128)(2,1)S(1)}, bf16[256,1536]{1,0:T(8,128)(2,1)}, u32[]{:S(2)}) copy-start(bf16[256,1536]{1,0:T(8,128)(2,1)} %copy-done.4) | copy-start | bytes 2359300 | tf_op jit(solution)/shard_map/while
  340.3 4.3 copy-start.4
  347.3 8.0 %copy-start.1 = (bf16[384,1536]{1,0:T(8,128)(2,1)S(1)}, bf16[384,1536]{1,0:T(8,128)(2,1)}, u32[]{:S(2)}) copy-start(bf16[384,1536]{1,0:T(8,128)(2,1)} %get-tuple-element.814) | copy-start | bytes 3538948 | tf_op jit(solution)/shard_map/while
  347.3 8.0 %copy-start.5 = (bf16[256,1536]{1,0:T(8,128)(2,1)S(1)}, bf16[256,1536]{1,0:T(8,128)(2,1)}, u32[]{:S(2)}) copy-start(bf16[256,1536]{1,0:T(8,128)(2,1)} %copy-done.4) | copy-start | bytes 2359300 | tf_op jit(solution)/shard_map/while
  362.3 8.0 %copy-start.1 = (bf16[384,1536]{1,0:T(8,128)(2,1)S(1)}, bf16[384,1536]{1,0:T(8,128)(2,1)}, u32[]{:S(2)}) copy-start(bf16[384,1536]{1,0:T(8,128)(2,1)} %get-tuple-element.814) | copy-start | bytes 3538948 | tf_op jit(solution)/shard_map/while
  362.4 8.0 %copy-start.5 = (bf16[256,1536]{1,0:T(8,128)(2,1)S(1)}, bf16[256,1536]{1,0:T(8,128)(2,1)}, u32[]{:S(2)}) copy-start(bf16[256,1536]{1,0:T(8,128)(2,1)} %copy-done.4) | copy-start | bytes 2359300 | tf_op jit(solution)/shard_map/while
  377.3 8.0 %copy-start.1 = (bf16[384,1536]{1,0:T(8,128)(2,1)S(1)}, bf16[384,1536]{1,0:T(8,128)(2,1)}, u32[]{:S(2)}) copy-start(bf16[384,1536]{1,0:T(8,128)(2,1)} %get-tuple-element.814) | copy-start | bytes 3538948 | tf_op jit(solution)/shard_map/while
  377.4 8.0 %copy-start.5 = (bf16[256,1536]{1,0:T(8,128)(2,1)S(1)}, bf16[256,1536]{1,0:T(8,128)(2,1)}, u32[]{:S(2)}) copy-start(bf16[256,1536]{1,0:T(8,128)(2,1)} %copy-done.4) | copy-start | bytes 2359300 | tf_op jit(solution)/shard_map/while
  385.3 4.3 copy-start.4
  392.3 8.0 %copy-start.1 = (bf16[384,1536]{1,0:T(8,128)(2,1)S(1)}, bf16[384,1536]{1,0:T(8,128)(2,1)}, u32[]{:S(2)}) copy-start(bf16[384,1536]{1,0:T(8,128)(2,1)} %get-tuple-element.814) | copy-start | bytes 3538948 | tf_op jit(solution)/shard_map/while
  392.4 8.0 %copy-start.5 = (bf16[256,1536]{1,0:T(8,128)(2,1)S(1)}, bf16[256,1536]{1,0:T(8,128)(2,1)}, u32[]{:S(2)}) copy-start(bf16[256,1536]{1,0:T(8,128)(2,1)} %copy-done.4) | copy-start | bytes 2359300 | tf_op jit(solution)/shard_map/while
  407.4 8.0 %copy-start.1 = (bf16[384,1536]{1,0:T(8,128)(2,1)S(1)}, bf16[384,1536]{1,0:T(8,128)(2,1)}, u32[]{:S(2)}) copy-start(bf16[384,1536]{1,0:T(8,128)(2,1)} %get-tuple-element.814) | copy-start | bytes 3538948 | tf_op jit(solution)/shard_map/while
  407.4 8.0 %copy-start.5 = (bf16[256,1536]{1,0:T(8,128)(2,1)S(1)}, bf16[256,1536]{1,0:T(8,128)(2,1)}, u32[]{:S(2)}) copy-start(bf16[256,1536]{1,0:T(8,128)(2,1)} %copy-done.4) | copy-start | bytes 2359300 | tf_op jit(solution)/shard_map/while
  436.6 110.4 %copy-start.6 = (f32[4096,12]{0,1:T(8,128)}, f32[4096,12]{0,1:T(8,128)S(1)}, u32[]{:S(2)}) copy-start(f32[4096,12]{0,1:T(8,128)S(1)} %all-gather) | copy-start | bytes 589828
  456.1 91.0 %copy-start.7 = (f32[4096,12]{0,1:T(8,128)}, f32[4096,12]{0,1:T(8,128)S(1)}, u32[]{:S(2)}) copy-start(f32[4096,12]{0,1:T(8,128)S(1)} %all-gather.1) | copy-start | bytes 589828
  550.0 16.3 %slice-start.1 = ((f32[4096,12]{0,1:T(8,128)}), f32[256,12]{0,1:T(8,128)S(1)}, s32[]{:S(2)}) async-start(f32[4096,12]{0,1:T(8,128)} %copy-done.6), calls=%async_computation.2 | async-start | bytes 32768 | tf_op jit(solution)/shard_map/slice | solution.py:21
  550.0 16.3 %slice-start.2 = ((f32[4096,12]{0,1:T(8,128)}), f32[256,12]{0,1:T(8,128)S(1)}, s32[]{:S(2)}) async-start(f32[4096,12]{0,1:T(8,128)} %copy-done.7), calls=%async_computation.3 | async-start | bytes 32768 | tf_op jit(solution)/shard_map/slice | solution.py:21
  (68 other events, 136.7 us)
Sparse Core Ops, SparseCore 0:
  415.5 131.4 all-gather.4
where the time goes:
time: 664 us; the launch traced here: 660 us
  blocking collectives  179 us (27%)
  waiting for transfers between devices  148 us (22%)
  matrix products  119 us (18%)
  local copies, waits for them, and re-layouts  107 us (16%)
  other arithmetic  68.2 us (10%)
  starting transfers between devices  21.5 us (3%)
  between operations  14.3 us (2%)
    all_gather x1, blocking collectives, on_device(): lax.all_gather(key_text, 'ctx', axis=0, tiled=True)  93.3 us
    all_gather x1, waiting for transfers between devices, combined_all(): pieces = jax.tree.map(lambda part: lax.all_gather(part, axis), value)  90.8 us
    ppermute x8, waiting for transfers between devices, shifted(): return lax.ppermute(shard, axis, pairs)  57.1 us
    add x15, other arithmetic, combine_parts(): acc_early * spread_heads(factor_early)  42.2 us
    all_gather x2, blocking collectives, combined_all(): pieces = jax.tree.map(lambda part: lax.all_gather(part, axis), value)  40.7 us
    dynamic_slice x45, local copies, waits for them, and re-layouts, combined_all(): lax.scan(lambda total, share: (join(total, share), None), head, tail)  30.1 us
    all_gather x1, blocking collectives, on_device(): lax.all_gather(value_text, 'ctx', axis=0, tiled=True)  24.4 us
    dot_general x12, matrix products, head_step(): jnp.einsum('tqk,kd->tqd', weight_text.astype(jnp.bfloat16), value_words,...  22.7 us
  transfers between devices with their start and end apart: 9, of which 3 were waited for; matrix products, arithmetic and copies ran while one was open for 1% of the time, Pallas kernels for 0%

commit v1 on v0

--- a/solution.py
+++ b/solution.py
@@ -8,6 +8,22 @@
 HD = 128
 NB = 3
 REACH = 2
+
+
+def ring_gather(x, axis, dim):
+    ways, here, step = (lax.axis_size(axis), lax.axis_index(axis), x.shape[dim])
+    shape = [n * ways if d == dim else n for d, n in enumerate(x.shape)]
+    full = lax.dynamic_update_slice_in_dim(jnp.zeros(shape, x.dtype), x, here * step, axis=dim)
+    going_up = going_down = x
+    for far in range(1, ways // 2 + 1):
+        going_up = lax.ppermute(going_up, axis, [(d, (d + 1) % ways) for d in range(ways)])
+        full = lax.dynamic_update_slice_in_dim(full, going_up, (here - far) % ways * step, axis=dim)
+        if 2 * far < ways:
+            going_down = lax.ppermute(going_down, axis, [(d, (d - 1) % ways) for d in range(ways)])
+            full = lax.dynamic_update_slice_in_dim(
+                full, going_down, (here + far) % ways * step, axis=dim
+            )
+    return full
 
 
 def shifted(shard, axis, by):
@@ -59,7 +75,7 @@
     text_query, text_keys, text_values = (
         lax.all_gather(query_text, "ctx", axis=0, tiled=True),
         lax.all_gather(key_text, "ctx", axis=0, tiled=True),
-        lax.all_gather(value_text, "ctx", axis=0, tiled=True),
+        ring_gather(value_text, "ctx", 0),
     )
     text_rows = text_keys.shape[0]
     text_limit = text_count[0]

time: 664 us -> 687 us (1.035)
  waiting for transfers between devices: 148 us -> 208 us
  blocking collectives: 179 us -> 140 us
  matrix products: 119 us -> 111 us
  local copies, waits for them, and re-layouts: 107 us -> 115 us
    ppermute x0 -> x15, waiting for transfers between devices: none -> 60.4 us  [the longest x8 34.7 us: ring_gather(): lax.ppermute(going_up, axis, [(d, (d + 1) % ways) for d in range(ways)])]
    all_gather x1, blocking collectives: 93.3 us -> 63.2 us  [on_device(): lax.all_gather(key_text, 'ctx', axis=0, tiled=True)]
    all_gather x1 -> x0, blocking collectives: 24.4 us -> none  [on_device(): lax.all_gather(value_text, 'ctx', axis=0, tiled=True)]
    all_gather x2, blocking collectives: 40.7 us -> 52.1 us  [combined_all(): pieces = jax.tree.map(lambda part: lax.all_gather(part, axis), value)]
    ppermute x0 -> x15, starting transfers between devices: none -> 10.2 us  [the longest x8 5.16 us: ring_gather(): lax.ppermute(going_up, axis, [(d, (d + 1) % ways) for d in range(ways)])]
    dynamic_update_slice x0 -> x16, local copies, waits for them, and re-layouts: none -> 9.9 us  [the longest x8 4.96 us: ring_gather(): lax.dynamic_update_slice_in_dim(full, going_up, (here - far) % ways * ste...]
    ppermute x8, starting transfers between devices: 21.5 us -> 12.5 us  [shifted(): return lax.ppermute(shard, axis, pairs)]
    dot_general x12, matrix products: 10.8 us -> 2.54 us  [head_step(): jnp.einsum('tk,kd->td', weight_own.astype(jnp.bfloat16), value_own_text,...]
  transfers between devices with their start and end apart: 9 -> 24, of which waited for: 3 -> 16; matrix products, arithmetic and copies ran while one was open for 1% -> 2% of each run, Pallas kernels for 0% -> 0%
where the time goes in v1:
time: 687 us; the launch traced here: 682 us
  waiting for transfers between devices  208 us (30%)
  blocking collectives  140 us (20%)
  local copies, waits for them, and re-layouts  115 us (17%)
  matrix products  111 us (16%)
  other arithmetic  68.7 us (10%)
  starting transfers between devices  22.8 us (3%)
  between operations  14.7 us (2%)
    all_gather x1, waiting for transfers between devices, combined_all(): pieces = jax.tree.map(lambda part: lax.all_gather(part, axis), value)  90.8 us
    all_gather x1, blocking collectives, on_device(): lax.all_gather(key_text, 'ctx', axis=0, tiled=True)  63.2 us
    ppermute x8, waiting for transfers between devices, shifted(): return lax.ppermute(shard, axis, pairs)  56.6 us
    all_gather x2, blocking collectives, combined_all(): pieces = jax.tree.map(lambda part: lax.all_gather(part, axis), value)  52.1 us
    add x15, other arithmetic, combine_parts(): acc_early * spread_heads(factor_early)  42.7 us
    ppermute x8, waiting for transfers between devices, ring_gather(): lax.ppermute(going_up, axis, [(d, (d + 1) % ways) for d in range(ways)])  34.7 us
    dynamic_slice x45, local copies, waits for them, and re-layouts, combined_all(): lax.scan(lambda total, share: (join(total, share), None), head, tail)  30.1 us
    ppermute x7, waiting for transfers between devices, ring_gather(): lax.ppermute(going_down, axis, [(d, (d - 1) % ways) for d in range(ways)])  25.8 us
  transfers between devices with their start and end apart: 24, of which 16 were waited for; matrix products, arithmetic and copies ran while one was open for 2% of the time, Pallas kernels for 0%

profile of v1, /device:TPU:0, one launch (start us, length us, event | category | flops | bytes accessed | tf_op | source)
XLA Modules:
  0.0 682.3 jit_solution(15692837529928406859)
XLA Ops:
  7.7 5.1 collective-permute-start.9
  12.8 2.3 collective-permute-start
  15.1 2.4 collective-permute-start.1
  18.8 63.2 %all_gather.24 = bf16[256,1536]{1,0:T(8,128)(2,1)S(1)} all-gather(bf16[16,1536]{1,0:T(8,128)(2,1)} %param.17), channel_id=1, replica_groups=mesh['groups'=2,'ctx'=16] {'ctx'}, dimensions={0}, use_global_device_ids=true | all-gather | bytes 835584 | tf_op jit(solution)/shard_map/all_gather | solution.py:77
  82.0 24.4 %all_gather.25 = bf16[256,1536]{1,0:T(8,128)(2,1)} all-gather(bf16[16,1536]{1,0:T(8,128)(2,1)} %param.16), channel_id=1, replica_groups=mesh['groups'=2,'ctx'=16] {'ctx'}, dimensions={0}, use_global_device_ids=true | all-gather | bytes 835584 | tf_op jit(solution)/shard_map/all_gather | solution.py:76
  111.5 5.3 collective-permute-done.10
  117.4 20.1 %collective-permute-done.11 = bf16[16,1536]{1,0:T(8,128)(2,1)S(1)} collective-permute-done((bf16[16,1536]{1,0:T(8,128)(2,1)S(1)}, bf16[16,1536]{1,0:T(8,128)(2,1)S(1)}, u32[]{:S(2)}, u32[]{:S(2)}) %collective-permute-start.11) | collective-permute-done | bytes 49184 | tf_op jit(solution)/shard_map/ppermute | solution.py:22
  137.5 3.5 collective-permute-start.12
  141.6 2.1 collective-permute-done.12
  146.9 4.9 collective-permute-done.14
  154.1 5.6 collective-permute-done.16
  162.1 5.6 collective-permute-done.18
  170.1 5.6 collective-permute-done.20
  178.1 5.6 collective-permute-done.22
  194.0 22.5 %collective-permute-done.3 = bf16[384,1536]{1,0:T(8,128)(2,1)S(1)} collective-permute-done((bf16[384,1536]{1,0:T(8,128)(2,1)S(1)}, bf16[384,1536]{1,0:T(8,128)(2,1)S(1)}, u32[]{:S(2)}, u32[]{:S(2)}) %collective-permute-start.3) | collective-permute-done | bytes 1179680 | tf_op jit(solution)/shard_map/ppermute | solution.py:32
  216.6 34.1 %collective-permute-done.7 = bf16[384,1536]{1,0:T(8,128)(2,1)S(1)} collective-permute-done((bf16[384,1536]{1,0:T(8,128)(2,1)}, bf16[384,1536]{1,0:T(8,128)(2,1)S(1)}, u32[]{:S(2)}, u32[]{:S(2)}) %collective-permute-start.7) | collective-permute-done | bytes 1179680 | tf_op jit(solution)/shard_map/ppermute | solution.py:32
  254.2 171.7 %while.36 = (s32[]{:T(128)}, bf16[384,1536]{1,0:T(8,128)(2,1)}, f32[256,12]{0,1:T(8,128)S(1)}, f32[256,12]{0,1:T(8,128)S(1)}, f32[256,1536]{1,0:T(8,128)}, /*ind...) while((s32[]{:T(128)}, bf16[384,1536]{1,0:T(8,128)(2,1)}, ...), condition=%wide.region_10.11_spmd.clone.clone, body=%wide.region_1.10_spmd.clone.clone.sunk | while | flops 333393952 | bytes 24062668 | solution.py:190
  261.2 1.9 fusion.103
  275.5 1.9 fusion.103
  289.8 1.9 fusion.103
  318.5 1.9 fusion.103
  332.8 1.9 fusion.103
  347.1 1.9 fusion.103
  361.4 1.9 fusion.103
  375.7 1.9 fusion.103
  404.3 1.9 fusion.103
  409.3 1.9 fusion.109
  418.6 1.9 fusion.103
  425.9 32.6 %all-gather = f32[4096,12]{0,1:T(8,128)S(1)} all-gather(f32[256,12]{0,1:T(8,128)S(1)} %get-tuple-element.794), channel_id=2, replica_groups=mesh['groups'=2,'ctx'=16] {'ctx'}, dimensions={0}, use_global_device_ids=true | all-gather | bytes 208896 | tf_op jit(solution)/shard_map/all_gather | solution.py:36
  458.6 19.5 %all-gather.1 = f32[4096,12]{0,1:T(8,128)S(1)} all-gather(f32[256,12]{0,1:T(8,128)S(1)} %get-tuple-element.795), channel_id=3, replica_groups=mesh['groups'=2,'ctx'=16] {'ctx'}, dimensions={0}, use_global_device_ids=true | all-gather | bytes 208896 | tf_op jit(solution)/shard_map/all_gather | solution.py:36
  478.2 90.8 %all-gather.5.cloned.1.call-done = f32[4096,1536]{1,0:T(8,128)} async-done(((f32[256,1536]{1,0:T(8,128)}), f32[4096,1536]{1,0:T(8,128)}) %all-gather.5.cloned.1.call-update) | async-done | bytes 25165840 | tf_op jit(solution)/shard_map/all_gather | solution.py:36
  572.0 16.3 %slice.39 = f32[3840,1536]{1,0:T(8,128)} slice(f32[4096,1536]{1,0:T(8,128)} %all-gather.5.cloned.1.call-done), slice={[256:4096], [0:1536]} | slice | bytes 47185920 | tf_op jit(solution)/shard_map/slice | solution.py:38
  588.3 84.3 %while.35 = (s32[]{:T(128)}, f32[256,12]{0,1:T(8,128)S(1)}, f32[256,12]{0,1:T(8,128)S(1)}, f32[256,1536]{0,1:T(8,128)}, f32[15,256,12]{1,0,2:T(8,128)S(1)}, /*in...) while((s32[]{:T(128)}, f32[256,12]{0,1:T(8,128)S(1)}, f32[256,12]{0,1:T(8,128)S(1)}, ...), condition=%wide.region_12.13_spmd, body=%wide.region_11.12_spmd.sunk | while | flops 1198082 | bytes 14131405 | solution.py:39
  591.1 2.8 fusion.87
  596.7 2.8 fusion.87
  602.3 2.8 fusion.87
  607.9 2.8 fusion.87
  613.6 2.8 fusion.87
  619.2 2.8 fusion.87
  624.8 2.8 fusion.87
  630.4 2.8 fusion.87
  636.0 2.8 fusion.87
  641.6 2.8 fusion.87
  647.3 2.8 fusion.87
  652.9 2.8 fusion.87
  658.5 2.8 fusion.87
  664.1 2.8 fusion.87
  669.7 2.8 fusion.87
  (640 shorter events, 230.0 us)
Async XLA Ops:
  7.2 100.2 %copy-start.12 = (bf16[16,1536]{1,0:T(8,128)(2,1)S(1)}, bf16[16,1536]{1,0:T(8,128)(2,1)}, u32[]{:S(2)}) copy-start(bf16[16,1536]{1,0:T(8,128)(2,1)} %param.18) | copy-start | bytes 147460
  7.2 100.8 %copy-start.13 = (s32[1,3]{1,0:T(1,128)S(1)}, s32[1,3]{1,0:T(1,128)}, u32[]{:S(2)}) copy-start(s32[1,3]{1,0:T(1,128)} %param.19) | copy-start | bytes 40
  7.2 100.8 %copy-start.14 = (s32[16]{0:T(128)S(1)}, s32[16]{0:T(128)}, u32[]{:S(2)}) copy-start(s32[16]{0:T(128)} %param.20) | copy-start | bytes 196
  7.2 561.8 %all-gather.5.cloned.1.call-start = ((), (), s32[]{:S(2)}) async-start(), calls=%async_computation | async-start | bytes 26738688 | tf_op jit(solution)/shard_map/all_gather | solution.py:36
  7.2 101.3 %collective-permute-start.8 = (bf16[16,1536]{1,0:T(8,128)(2,1)}, bf16[16,1536]{1,0:T(8,128)(2,1)S(1)}, u32[]{:S(2)}, u32[]{:S(2)}) collective-permute-start(bf16[16,1536]{1,0:T(8,128)(2,1)} %param.18), channel_id=1, source_target_pairs={{0,1},{1,2},{2,3},{3,4},{4,5},{5,6},{6,7},{7,8},{8,9},{9,10},{10,1... | collective-permute-start | bytes 147464 | tf_op jit(solution)/shard_map/ppermute | solution.py:19
  7.7 102.8 %collective-permute-start.9 = (bf16[16,1536]{1,0:T(8,128)(2,1)}, bf16[16,1536]{1,0:T(8,128)(2,1)S(1)}, u32[]{:S(2)}, u32[]{:S(2)}) collective-permute-start(bf16[16,1536]{1,0:T(8,128)(2,1)} %param.18), channel_id=1, source_target_pairs={{0,15},{1,0},{2,1},{3,2},{4,3},{5,4},{6,5},{7,6},{8,7},{9,8},{10,9... | collective-permute-start | bytes 147464 | tf_op jit(solution)/shard_map/ppermute | solution.py:22
  12.8 172.9 %collective-permute-start = (bf16[384,1536]{1,0:T(8,128)(2,1)}, bf16[384,1536]{1,0:T(8,128)(2,1)}, u32[]{:S(2)}, u32[]{:S(2)}) collective-permute-start(bf16[384,1536]{1,0:T(8,128)(2,1)} %param.14), channel_id=1, source_target_pairs={{0,2},{1,3},{2,4},{3,5},{4,6},{5,7},{6,8},{7,9},{8,10},{9,11},{10,... | collective-permute-start | bytes 3538952 | tf_op jit(solution)/shard_map/ppermute | solution.py:32
  15.1 173.2 %collective-permute-start.1 = (bf16[384,1536]{1,0:T(8,128)(2,1)}, bf16[384,1536]{1,0:T(8,128)(2,1)}, u32[]{:S(2)}, u32[]{:S(2)}) collective-permute-start(bf16[384,1536]{1,0:T(8,128)(2,1)} %param.14), channel_id=1, source_target_pairs={{0,1},{1,2},{2,3},{3,4},{4,5},{5,6},{6,7},{7,8},{8,9},{9,10},{10,1... | collective-permute-start | bytes 3538952 | tf_op jit(solution)/shard_map/ppermute | solution.py:32
  17.5 176.4 %collective-permute-start.2 = (bf16[384,1536]{1,0:T(8,128)(2,1)}, bf16[384,1536]{1,0:T(8,128)(2,1)S(1)}, u32[]{:S(2)}, u32[]{:S(2)}) collective-permute-start(bf16[384,1536]{1,0:T(8,128)(2,1)} %param.14), channel_id=1, source_target_pairs={{1,0},{2,1},{3,2},{4,3},{5,4},{6,5},{7,6},{8,7},{9,8},{10,9},{11,1... | collective-permute-start | bytes 3538952 | tf_op jit(solution)/shard_map/ppermute | solution.py:32
  106.4 79.3 %copy-start = (bf16[384,1536]{1,0:T(8,128)(2,1)S(1)}, bf16[384,1536]{1,0:T(8,128)(2,1)}, u32[]{:S(2)}) copy-start(bf16[384,1536]{1,0:T(8,128)(2,1)} %param.14) | copy-start | bytes 3538948
  108.5 82.5 %collective-permute-start.4 = (bf16[384,1536]{1,0:T(8,128)(2,1)}, bf16[384,1536]{1,0:T(8,128)(2,1)S(1)}, u32[]{:S(2)}, u32[]{:S(2)}) collective-permute-start(bf16[384,1536]{1,0:T(8,128)(2,1)} %param.15), channel_id=1, source_target_pairs={{0,2},{1,3},{2,4},{3,5},{4,6},{5,7},{6,8},{7,9},{8,10},{9,11},{10,... | collective-permute-start | bytes 3538952 | tf_op jit(solution)/shard_map/ppermute | solution.py:32
  110.5 6.2 collective-permute-start.10
  116.8 20.7 %collective-permute-start.11 = (bf16[16,1536]{1,0:T(8,128)(2,1)S(1)}, bf16[16,1536]{1,0:T(8,128)(2,1)S(1)}, u32[]{:S(2)}, u32[]{:S(2)}) collective-permute-start(bf16[16,1536]{1,0:T(8,128)(2,1)S(1)} %collective-permute-done.9), channel_id=1, source_target_pairs={{0,15},{1,0},{2,1},{3,2},{4,3},{5,4},{6,5},{7,6},{8,7},{9,8},{10,9... | collective-permute-start | bytes 147464 | tf_op jit(solution)/shard_map/ppermute | solution.py:22
  137.5 6.2 collective-permute-start.12
  143.7 1.8 collective-permute-start.13
  145.4 6.3 collective-permute-start.14
  151.7 1.8 collective-permute-start.15
  153.5 6.2 collective-permute-start.16
  159.7 1.8 collective-permute-start.17
  161.5 6.2 collective-permute-start.18
  167.7 1.8 collective-permute-start.19
  169.4 6.2 collective-permute-start.20
  175.7 1.8 collective-permute-start.21
  177.4 6.2 collective-permute-start.22
  183.7 8.8 %collective-permute-start.5 = (bf16[384,1536]{1,0:T(8,128)(2,1)}, bf16[384,1536]{1,0:T(8,128)(2,1)S(1)}, u32[]{:S(2)}, u32[]{:S(2)}) collective-permute-start(bf16[384,1536]{1,0:T(8,128)(2,1)} %param.15), channel_id=1, source_target_pairs={{0,1},{1,2},{2,3},{3,4},{4,5},{5,6},{6,7},{7,8},{8,9},{9,10},{10,1... | collective-permute-start | bytes 3538952 | tf_op jit(solution)/shard_map/ppermute | solution.py:32
  185.7 30.8 %collective-permute-start.3 = (bf16[384,1536]{1,0:T(8,128)(2,1)S(1)}, bf16[384,1536]{1,0:T(8,128)(2,1)S(1)}, u32[]{:S(2)}, u32[]{:S(2)}) collective-permute-start(bf16[384,1536]{1,0:T(8,128)(2,1)S(1)} %copy-done), channel_id=1, source_target_pairs={{2,0},{3,1},{4,2},{5,3},{6,4},{7,5},{8,6},{9,7},{10,8},{11,9},{12,... | collective-permute-start | bytes 3538952 | tf_op jit(solution)/shard_map/ppermute | solution.py:32
  188.3 28.2 %collective-permute-start.6 = (bf16[384,1536]{1,0:T(8,128)(2,1)}, bf16[384,1536]{1,0:T(8,128)(2,1)S(1)}, u32[]{:S(2)}, u32[]{:S(2)}) collective-permute-start(bf16[384,1536]{1,0:T(8,128)(2,1)} %param.15), channel_id=1, source_target_pairs={{1,0},{2,1},{3,2},{4,3},{5,4},{6,5},{7,6},{8,7},{9,8},{10,9},{11,1... | collective-permute-start | bytes 3538952 | tf_op jit(solution)/shard_map/ppermute | solution.py:32
  191.1 59.7 %collective-permute-start.7 = (bf16[384,1536]{1,0:T(8,128)(2,1)}, bf16[384,1536]{1,0:T(8,128)(2,1)S(1)}, u32[]{:S(2)}, u32[]{:S(2)}) collective-permute-start(bf16[384,1536]{1,0:T(8,128)(2,1)} %param.15), channel_id=1, source_target_pairs={{2,0},{3,1},{4,2},{5,3},{6,4},{7,5},{8,6},{9,7},{10,8},{11,9},{12,... | collective-permute-start | bytes 3538952 | tf_op jit(solution)/shard_map/ppermute | solution.py:32
  216.5 37.5 %copy-start.2 = (bf16[1920,1536]{1,0:T(8,128)(2,1)}, bf16[1920,1536]{1,0:T(8,128)(2,1)S(1)}, u32[]{:S(2)}) copy-start(bf16[1920,1536]{1,0:T(8,128)(2,1)S(1)} %constant_dynamic-update-slice_fusion) | copy-start | bytes 17694724
  289.8 7.3 %copy-start.1 = (bf16[384,1536]{1,0:T(8,128)(2,1)S(1)}, bf16[384,1536]{1,0:T(8,128)(2,1)}, u32[]{:S(2)}) copy-start(bf16[384,1536]{1,0:T(8,128)(2,1)} %get-tuple-element.814) | copy-start | bytes 3538948 | tf_op jit(solution)/shard_map/while
  289.8 7.3 %copy-start.5 = (bf16[256,1536]{1,0:T(8,128)(2,1)S(1)}, bf16[256,1536]{1,0:T(8,128)(2,1)}, u32[]{:S(2)}) copy-start(bf16[256,1536]{1,0:T(8,128)(2,1)} %copy-done.4) | copy-start | bytes 2359300 | tf_op jit(solution)/shard_map/while
  304.1 7.3 %copy-start.1 = (bf16[384,1536]{1,0:T(8,128)(2,1)S(1)}, bf16[384,1536]{1,0:T(8,128)(2,1)}, u32[]{:S(2)}) copy-start(bf16[384,1536]{1,0:T(8,128)(2,1)} %get-tuple-element.814) | copy-start | bytes 3538948 | tf_op jit(solution)/shard_map/while
  318.4 7.3 %copy-start.1 = (bf16[384,1536]{1,0:T(8,128)(2,1)S(1)}, bf16[384,1536]{1,0:T(8,128)(2,1)}, u32[]{:S(2)}) copy-start(bf16[384,1536]{1,0:T(8,128)(2,1)} %get-tuple-element.814) | copy-start | bytes 3538948 | tf_op jit(solution)/shard_map/while
  318.4 7.3 %copy-start.5 = (bf16[256,1536]{1,0:T(8,128)(2,1)S(1)}, bf16[256,1536]{1,0:T(8,128)(2,1)}, u32[]{:S(2)}) copy-start(bf16[256,1536]{1,0:T(8,128)(2,1)} %copy-done.4) | copy-start | bytes 2359300 | tf_op jit(solution)/shard_map/while
  347.0 7.3 %copy-start.1 = (bf16[384,1536]{1,0:T(8,128)(2,1)S(1)}, bf16[384,1536]{1,0:T(8,128)(2,1)}, u32[]{:S(2)}) copy-start(bf16[384,1536]{1,0:T(8,128)(2,1)} %get-tuple-element.814) | copy-start | bytes 3538948 | tf_op jit(solution)/shard_map/while
  347.0 7.3 %copy-start.5 = (bf16[256,1536]{1,0:T(8,128)(2,1)S(1)}, bf16[256,1536]{1,0:T(8,128)(2,1)}, u32[]{:S(2)}) copy-start(bf16[256,1536]{1,0:T(8,128)(2,1)} %copy-done.4) | copy-start | bytes 2359300 | tf_op jit(solution)/shard_map/while
  361.3 7.3 %copy-start.1 = (bf16[384,1536]{1,0:T(8,128)(2,1)S(1)}, bf16[384,1536]{1,0:T(8,128)(2,1)}, u32[]{:S(2)}) copy-start(bf16[384,1536]{1,0:T(8,128)(2,1)} %get-tuple-element.814) | copy-start | bytes 3538948 | tf_op jit(solution)/shard_map/while
  361.4 7.3 %copy-start.5 = (bf16[256,1536]{1,0:T(8,128)(2,1)S(1)}, bf16[256,1536]{1,0:T(8,128)(2,1)}, u32[]{:S(2)}) copy-start(bf16[256,1536]{1,0:T(8,128)(2,1)} %copy-done.4) | copy-start | bytes 2359300 | tf_op jit(solution)/shard_map/while
  375.7 7.3 %copy-start.1 = (bf16[384,1536]{1,0:T(8,128)(2,1)S(1)}, bf16[384,1536]{1,0:T(8,128)(2,1)}, u32[]{:S(2)}) copy-start(bf16[384,1536]{1,0:T(8,128)(2,1)} %get-tuple-element.814) | copy-start | bytes 3538948 | tf_op jit(solution)/shard_map/while
  375.7 7.3 %copy-start.5 = (bf16[256,1536]{1,0:T(8,128)(2,1)S(1)}, bf16[256,1536]{1,0:T(8,128)(2,1)}, u32[]{:S(2)}) copy-start(bf16[256,1536]{1,0:T(8,128)(2,1)} %copy-done.4) | copy-start | bytes 2359300 | tf_op jit(solution)/shard_map/while
  404.3 7.3 %copy-start.1 = (bf16[384,1536]{1,0:T(8,128)(2,1)S(1)}, bf16[384,1536]{1,0:T(8,128)(2,1)}, u32[]{:S(2)}) copy-start(bf16[384,1536]{1,0:T(8,128)(2,1)} %get-tuple-element.814) | copy-start | bytes 3538948 | tf_op jit(solution)/shard_map/while
  404.3 7.3 %copy-start.5 = (bf16[256,1536]{1,0:T(8,128)(2,1)S(1)}, bf16[256,1536]{1,0:T(8,128)(2,1)}, u32[]{:S(2)}) copy-start(bf16[256,1536]{1,0:T(8,128)(2,1)} %copy-done.4) | copy-start | bytes 2359300 | tf_op jit(solution)/shard_map/while
  418.6 7.3 %copy-start.1 = (bf16[384,1536]{1,0:T(8,128)(2,1)S(1)}, bf16[384,1536]{1,0:T(8,128)(2,1)}, u32[]{:S(2)}) copy-start(bf16[384,1536]{1,0:T(8,128)(2,1)} %get-tuple-element.814) | copy-start | bytes 3538948 | tf_op jit(solution)/shard_map/while
  418.6 7.3 %copy-start.5 = (bf16[256,1536]{1,0:T(8,128)(2,1)S(1)}, bf16[256,1536]{1,0:T(8,128)(2,1)}, u32[]{:S(2)}) copy-start(bf16[256,1536]{1,0:T(8,128)(2,1)} %copy-done.4) | copy-start | bytes 2359300 | tf_op jit(solution)/shard_map/while
  458.5 110.4 %copy-start.6 = (f32[4096,12]{0,1:T(8,128)}, f32[4096,12]{0,1:T(8,128)S(1)}, u32[]{:S(2)}) copy-start(f32[4096,12]{0,1:T(8,128)S(1)} %all-gather) | copy-start | bytes 589828
  478.0 91.0 %copy-start.7 = (f32[4096,12]{0,1:T(8,128)}, f32[4096,12]{0,1:T(8,128)S(1)}, u32[]{:S(2)}) copy-start(f32[4096,12]{0,1:T(8,128)S(1)} %all-gather.1) | copy-start | bytes 589828
  572.0 16.3 %slice-start.1 = ((f32[4096,12]{0,1:T(8,128)}), f32[256,12]{0,1:T(8,128)S(1)}, s32[]{:S(2)}) async-start(f32[4096,12]{0,1:T(8,128)} %copy-done.6), calls=%async_computation.2 | async-start | bytes 32768 | tf_op jit(solution)/shard_map/slice | solution.py:37
  572.0 16.3 %slice-start.2 = ((f32[4096,12]{0,1:T(8,128)}), f32[256,12]{0,1:T(8,128)S(1)}, s32[]{:S(2)}) async-start(f32[4096,12]{0,1:T(8,128)} %copy-done.7), calls=%async_computation.3 | async-start | bytes 32768 | tf_op jit(solution)/shard_map/slice | solution.py:37
  (83 other events, 228.8 us)
Sparse Core Ops, SparseCore 0:
  426.0 142.8 all-gather.4
